TPU v7x, 32 devices: a whole 2x2x4 slice. The times are simulated.
32 devices in a mesh: tok: 8 (over y, x, core), lat: 4 (over z).
Axes of the slice: x: 2, y: 2, z: 4, core: 2. Of those that a mesh axis runs over, the one named last changes fastest.
Arguments:
- captured: bfloat16 [1024, 16384], P(None, 'tok'), may hold values from -6 to 6
- enc_weight: bfloat16 [16384, 16384], P('tok', 'lat'), may hold values from -0.046875 to 0.046875
- enc_bias: float32 [16384], P('lat'), may hold values from -3 to 3
- dec_weight: bfloat16 [16384, 16384], P('lat', 'tok'), may hold values from -0.1875 to 0.1875
- dec_bias: float32 [16384], P('tok'), may hold values from -1.5 to 1.5
- block_ids: int32 [8, 4, 2], P(None, 'lat'), may hold values from 0 to 31, as said below
- block_counts: int32 [8, 4], P(None, 'lat'), may hold values from 1 to 2, as said below
Outputs:
- enc_grad: bfloat16 [16384, 16384], P('tok', 'lat')
- dec_grad: bfloat16 [16384, 16384], P('lat', 'tok')
Inputs may be any that keep to these rules, and one draw needn't show every extreme that they name: block_ids[b, s, k] numbers a latent block within latent shard s; the 2 entries of one token block and shard are distinct, and those with k >= block_counts[b, s] are inactive slots. block_counts[b, s] is how many leading slots of block_ids[b, s] are active; some entry equals 2 in every draw.
All inputs are finite; a program needn't handle non-finite values.
Results may differ from a plain program's by a relative error of at most 0.02.
Values may be sent and summed in bfloat16 or wider, within the bound.
A program may use at most 192 MiB of HBM per device.

v0:
```python
import functools

import jax
import jax.numpy as jnp
from jax import lax
from jax.experimental import pallas as pl
from jax.experimental.pallas import tpu as pltpu
from jax.sharding import PartitionSpec as P

TB = 128
LB = 128
KS = 2

SCALE_ERR = 0.0625
PENALTY = 0.05
F32 = jnp.float32
BF16 = jnp.bfloat16
MESH = pl.DeviceIdType.MESH
VMEM = pltpu.VMEM
BIG = 60 * 1024 * 1024


def dot(a, b, ca, cb):
    return lax.dot_general(a, b, (((ca,), (cb,)), ((), ())), preferred_element_type=F32)


def pre_kernel(ids, counts, cap_ref, *refs):
    enc_refs, bias_refs = refs[:KS], refs[KS:2 * KS]
    pre_ref, bsel_ref, live_ref, order_ref, tile_ref, first_ref, place = refs[2 * KS:]
    b = pl.program_id(0)

    @pl.when(b == 0)
    def _():
        def clear(g, carry):
            place[g] = 0
            return carry

        def count(s, carry):
            place[ids[s]] += 1
            return carry

        def unnamed(g, at):
            @pl.when(place[g] == 0)
            def _():
                tile_ref[at] = g

            return at + (place[g] == 0).astype(jnp.int32)

        def taken(g, at):
            @pl.when(place[g] > 0)
            def _():
                tile_ref[at] = g

            return at + (place[g] > 0).astype(jnp.int32)

        def offset(g, seen):
            here = place[g]
            place[g] = seen
            first_ref[g] = seen
            return seen + here

        def put(s, carry):
            at = place[ids[s]]
            order_ref[at] = s
            place[ids[s]] = at + 1
            return carry

        slots, groups = order_ref.shape[0], place.shape[0]
        lax.fori_loop(0, groups, clear, 0)
        lax.fori_loop(0, slots, count, 0)
        lax.fori_loop(0, groups, taken, lax.fori_loop(0, groups, unnamed, jnp.int32(0)))
        first_ref[groups] = lax.fori_loop(0, groups, offset, jnp.int32(0))
        lax.fori_loop(0, slots, put, 0)

    tiles = jnp.concatenate([r[...] for r in enc_refs], axis=1)
    pre = dot(cap_ref[...], tiles, 1, 0).astype(BF16)
    for k in range(KS):
        pre_ref[k * TB:(k + 1) * TB] = pre[:, k * LB:(k + 1) * LB]
        bsel_ref[k] = bias_refs[k][0]
        live_ref[k] = jnp.full((1, LB), (k < counts[b]).astype(F32), F32)


def named(k, place):
    return lambda b, ids, counts: place(ids[b * KS + k])


def partial_pre(ids, counts, captured, enc_weight, enc_bias):
    features = captured.shape[1]
    slots = ids.shape[0]
    groups = enc_weight.shape[1] // LB
    step = lambda b, ids, counts: (b, 0)
    row = pl.BlockSpec((KS, 1, LB), lambda b, ids, counts: (b, 0, 0))
    return pl.pallas_call(
        pre_kernel,
        grid_spec=pltpu.PrefetchScalarGridSpec(
            num_scalar_prefetch=2,
            grid=(slots // KS,),
            in_specs=[pl.BlockSpec((TB, features), step)]
            + [pl.BlockSpec((features, LB), named(k, lambda g: (0, g))) for k in range(KS)]
            + [pl.BlockSpec((1, 1, LB), named(k, lambda g: (g, 0, 0))) for k in range(KS)],
            out_specs=[
                pl.BlockSpec((KS * TB, LB), step), row, row,
            ] + [pl.BlockSpec(memory_space=pltpu.SMEM)] * 3,
            scratch_shapes=[pltpu.SMEM((groups,), jnp.int32)],
        ),
        out_shape=[
            jax.ShapeDtypeStruct((slots * TB, LB), BF16),
            jax.ShapeDtypeStruct((slots, 1, LB), F32),
            jax.ShapeDtypeStruct((slots, 1, LB), F32),
            jax.ShapeDtypeStruct((slots,), jnp.int32),
            jax.ShapeDtypeStruct((groups,), jnp.int32),
            jax.ShapeDtypeStruct((groups + 1,), jnp.int32),
        ],
        compiler_params=pltpu.CompilerParams(vmem_limit_bytes=BIG),
        name="partial_pre",
    )(
        ids, counts, captured, *([enc_weight] * KS), *([enc_bias.reshape(-1, 1, LB)] * KS),
    )


def middle_kernel(
    n, nz, chunk, lag,
    ids, pre_ref, bias_ref, live_ref, dbias_ref, cap_hbm, dec_hbm,
    codes_ref, dpre_ref, delta_hbm,
    cap_v, dec_v, part_v, delta_v, up_in, down_in, up_out, down_out,
    pre_in, dc_out, dc_in,
    up_send, up_recv, down_send, down_recv,
    pre_send, pre_recv, code_send, code_recv, dc_send, dc_recv, dp_send, dp_recv,
    load_sem, store_sem,
):
    me = lax.axis_index("tok")
    z = lax.axis_index("lat")
    group = part_v.shape[0] // n
    per = group // chunk
    own = group // TB
    chunks = n * per
    has_low = z > 0
    has_high = z < nz - 1
    inner = jnp.logical_and(has_low, has_high)
    low = jnp.maximum(z - 1, 0)
    high = jnp.minimum(z + 1, nz - 1)

    load_dec = pltpu.make_async_copy(dec_hbm, dec_v, load_sem.at[0])
    load_cap = pltpu.make_async_copy(cap_hbm, cap_v, load_sem.at[1])
    load_dec.start()
    load_cap.start()

    barrier = pltpu.get_barrier_semaphore()
    for d in range(1, n):
        pl.semaphore_signal(barrier, inc=1, device_id={"tok": lax.rem(me + d, n)}, device_id_type=MESH)

    @pl.when(has_low)
    def _():
        pl.semaphore_signal(barrier, inc=1, device_id={"lat": low}, device_id_type=MESH)

    @pl.when(has_high)
    def _():
        pl.semaphore_signal(barrier, inc=1, device_id={"lat": high}, device_id_type=MESH)

    pl.semaphore_wait(barrier, n - 1 + has_low.astype(jnp.int32) + has_high.astype(jnp.int32))

    def tok_copy(src, dst, send, recv, d, peer):
        return pltpu.make_async_remote_copy(
            src_ref=src, dst_ref=dst, send_sem=send.at[d - 1], recv_sem=recv.at[d - 1],
            device_id={"tok": peer}, device_id_type=MESH,
        )

    outgoing = []
    for d in range(1, n):
        peer = lax.rem(me + d, n)
        copy = tok_copy(pre_ref.at[peer], pre_in.at[d - 1], pre_send, pre_recv, d, peer)
        copy.start()
        outgoing.append(copy)
    for copy in outgoing:
        copy.wait()
    total = pre_ref[me].astype(F32)
    for d in range(1, n):
        total = total + pre_in[d - 1].astype(F32)
    outs = []
    for s in range(own * KS):
        v = total[s * TB:(s + 1) * TB] + bias_ref[me * own * KS + s]
        soft = jnp.maximum(v, 0.0) + jnp.log1p(jnp.exp(-jnp.abs(v)))
        outs.append((soft * live_ref[me * own * KS + s]).astype(BF16))
    codes_ref[me] = jnp.concatenate(outs, axis=0)

    def give_codes(d):
        return tok_copy(codes_ref.at[me], codes_ref.at[me], code_send, code_recv, d, lax.rem(me + n - d, n))

    def get_codes(d, g):
        return tok_copy(codes_ref.at[g], codes_ref.at[g], code_send, code_recv, d, lax.rem(me + n - d, n))

    for d in range(1, n):
        give_codes(d).start()
    load_dec.wait()
    load_cap.wait()

    def group_of(i):
        return lax.rem(me + i, n)

    def rows(c):
        return pl.ds(pl.multiple_of(group_of(c // per) * group + lax.rem(c, per) * chunk, chunk), chunk)

    def line_copy(src, dst, send, recv, c, dev):
        return pltpu.make_async_remote_copy(
            src_ref=src.at[rows(c)], dst_ref=dst.at[rows(c)], send_sem=send.at[c], recv_sem=recv.at[c],
            device_id={"lat": dev}, device_id_type=MESH,
        )

    def up(c):
        return line_copy(up_out, up_in, up_send, up_recv, c, high)

    def up_first(c):
        return line_copy(part_v, up_in, up_send, up_recv, c, high)

    def down(c):
        return line_copy(down_out, down_in, down_send, down_recv, c, low)

    def down_first(c):
        return line_copy(part_v, down_in, down_send, down_recv, c, low)

    def block_rows(g, o, size):
        return pl.ds(pl.multiple_of((g * own + o) * size, size), size)

    def dec_tile(g, o):
        first = (g * own + o) * KS
        return jnp.concatenate([dec_v[ids[first + k]] for k in range(KS)], axis=0)

    def make_part(g):
        for o in range(own):
            tiles = [codes_ref[g, pl.ds((o * KS + k) * TB, TB)] for k in range(KS)]
            value = dot(jnp.concatenate(tiles, axis=1), dec_tile(g, o), 1, 0)
            part_v[block_rows(g, o, TB)] = value.astype(BF16)

    def delta_copy(g):
        span = pl.ds(pl.multiple_of(g * group, group), group)
        return pltpu.make_async_copy(delta_v.at[span], delta_hbm.at[span], store_sem.at[g])

    def give_dcodes(i):
        g = group_of(i)
        return tok_copy(dc_out.at[g], dc_in.at[i - 1], dc_send, dc_recv, i, g)

    up_delay = lag * z
    down_delay = lag * (nz - 1 - z)
    first_delay = jnp.minimum(up_delay, down_delay)
    last_delay = jnp.maximum(up_delay, down_delay)

    def step(t, carry):
        cf = t - first_delay
        cu = t - up_delay
        cd = t - down_delay
        cl = t - last_delay
        stage = jnp.maximum(cf, 0) // per

        @pl.when(jnp.logical_and(jnp.logical_and(cf >= 0, cf < chunks), lax.rem(jnp.maximum(cf, 0), per) == 0))
        def _():
            @pl.when(stage > 0)
            def _():
                get_codes(stage, group_of(stage)).wait_recv()

            make_part(group_of(stage))

        @pl.when(jnp.logical_and(cu >= 0, cu < chunks))
        def _():
            @pl.when(has_low)
            def _():
                up(cu).wait_recv()

                @pl.when(has_high)
                def _():
                    up_out[rows(cu)] = (up_in[rows(cu)].astype(F32) + part_v[rows(cu)].astype(F32)).astype(BF16)
                    up(cu).start()

            @pl.when(jnp.logical_not(has_low))
            def _():
                up_first(cu).start()

        @pl.when(jnp.logical_and(cd >= 0, cd < chunks))
        def _():
            @pl.when(has_high)
            def _():
                down(cd).wait_recv()

                @pl.when(has_low)
                def _():
                    down_out[rows(cd)] = (down_in[rows(cd)].astype(F32) + part_v[rows(cd)].astype(F32)).astype(BF16)
                    down(cd).start()

            @pl.when(jnp.logical_not(has_high))
            def _():
                down_first(cd).start()

        @pl.when(jnp.logical_and(cl >= 0, cl < chunks))
        def _():
            here = part_v[rows(cl)].astype(F32) + dbias_ref[...] - cap_v[rows(cl)].astype(F32)

            @pl.when(inner)
            def _():
                both = up_in[rows(cl)].astype(F32) + down_in[rows(cl)].astype(F32)
                delta_v[rows(cl)] = (SCALE_ERR * (here + both)).astype(BF16)

            @pl.when(jnp.logical_not(has_low))
            def _():
                delta_v[rows(cl)] = (SCALE_ERR * (here + down_in[rows(cl)].astype(F32))).astype(BF16)

            @pl.when(jnp.logical_not(has_high))
            def _():
                delta_v[rows(cl)] = (SCALE_ERR * (here + up_in[rows(cl)].astype(F32))).astype(BF16)

            done = cl // per

            @pl.when(lax.rem(cl, per) == per - 1)
            def _():
                g = group_of(done)
                for o in range(own):
                    value = dot(delta_v[block_rows(g, o, TB)], dec_tile(g, o), 1, 1).astype(BF16)
                    for k in range(KS):
                        dc_out[g, pl.ds((o * KS + k) * TB, TB)] = value[:, k * LB:(k + 1) * LB]

                @pl.when(done > 0)
                def _():
                    give_dcodes(done).start()

                delta_copy(g).start()

        return carry

    lax.fori_loop(0, chunks + lag * (nz - 1), step, 0)

    total = dc_out[me].astype(F32)
    for d in range(1, n):
        give_dcodes(d).wait_recv()
        total = total + dc_in[d - 1].astype(F32)
    dpre_ref[me] = ((total + PENALTY) * (1.0 - jnp.exp(-codes_ref[me].astype(F32)))).astype(BF16)

    def give_dpre(d, g):
        return tok_copy(dpre_ref.at[g], dpre_ref.at[g], dp_send, dp_recv, d, lax.rem(me + n - d, n))

    for d in range(1, n):
        give_dpre(d, me).start()

    def drain(c, carry):
        @pl.when(has_high)
        def _():
            up(c).wait_send()

        @pl.when(has_low)
        def _():
            down(c).wait_send()

        return carry

    lax.fori_loop(0, chunks, drain, 0)
    for g in range(n):
        delta_copy(g).wait()
    for d in range(1, n):
        give_codes(d).wait_send()
        give_dcodes(d).wait_send()
        give_dpre(d, me).wait_send()
        give_dpre(d, group_of(d)).wait_recv()


def middle(ids, pre, bias, live, dec_bias, captured, dec_weight, chunk, lag):
    n = lax.axis_size("tok")
    nz = lax.axis_size("lat")
    tokens, features = captured.shape
    rows = pre.shape[0] // n
    lat_dev = dec_weight.shape[0]
    chunks = tokens // chunk
    whole = pl.BlockSpec(memory_space=VMEM)
    outside = pl.BlockSpec(memory_space=pltpu.HBM)
    sems = lambda count: [pltpu.SemaphoreType.DMA((count,))]
    wide = VMEM((tokens, features), BF16)
    return pl.pallas_call(
        functools.partial(middle_kernel, n, nz, chunk, lag),
        out_shape=[
            jax.ShapeDtypeStruct((n, rows, LB), BF16),
            jax.ShapeDtypeStruct((n, rows, LB), BF16),
            jax.ShapeDtypeStruct((tokens, features), BF16),
        ],
        in_specs=[pl.BlockSpec(memory_space=pltpu.SMEM)] + [whole] * 4 + [outside] * 2,
        out_specs=[whole, whole, outside],
        scratch_shapes=[wide, VMEM((lat_dev // LB, LB, features), BF16)] + [wide] * 6
        + [VMEM((n - 1, rows, LB), BF16), VMEM((n, rows, LB), BF16), VMEM((n - 1, rows, LB), BF16)]
        + sems(chunks) * 4 + sems(n - 1) * 8 + sems(2) + sems(n),
        compiler_params=pltpu.CompilerParams(
            collective_id=0, has_side_effects=True, vmem_limit_bytes=BIG
        ),
        name="middle",
    )(
        ids, pre.reshape(n, rows, LB), bias, live, dec_bias.reshape(1, features), captured,
        dec_weight.reshape(-1, LB, features),
    )


def grads_kernel(
    order, tile, first, delta_hbm, codes_ref, cap_hbm, dpre_ref,
    enc_ref, dec_ref, delta_v, cap_v, dec_acc, enc_acc, state, delta_sem, cap_sem,
):
    i = pl.program_id(0)
    start = first[tile[i]]
    stop = first[tile[i] + 1]

    def loads(b):
        span = pl.ds(pl.multiple_of(b * TB, TB), TB)
        return (
            pltpu.make_async_copy(delta_hbm.at[span], delta_v.at[span], delta_sem.at[b]),
            pltpu.make_async_copy(cap_hbm.at[span], cap_v.at[span], cap_sem.at[b]),
        )

    @pl.when(i == 0)
    def _():
        def clear(b, carry):
            state[b] = 0
            return carry

        def begin(t, carry):
            b = order[t] // KS

            @pl.when(state[b] == 0)
            def _():
                for copy in loads(b):
                    copy.start()
                state[b] = 1

            return carry

        lax.fori_loop(0, state.shape[0], clear, 0)
        lax.fori_loop(0, order.shape[0], begin, 0)

    def tiles(t):
        s = order[t]
        b = s // KS

        @pl.when(state[b] == 1)
        def _():
            for copy in loads(b):
                copy.wait()
            state[b] = 2

        tokens = pl.ds(pl.multiple_of(b * TB, TB), TB)
        mine = pl.ds(pl.multiple_of(s * TB, TB), TB)
        return (
            dot(codes_ref[mine], delta_v[tokens], 0, 0),
            dot(cap_v[tokens], dpre_ref[mine], 0, 0),
        )

    @pl.when(stop == start)
    def _():
        dec_ref[...] = jnp.zeros(dec_ref.shape, BF16)
        enc_ref[...] = jnp.zeros(enc_ref.shape, BF16)

    @pl.when(stop == start + 1)
    def _():
        d, e = tiles(start)
        dec_ref[...] = d.astype(BF16)
        enc_ref[...] = e.astype(BF16)

    @pl.when(stop > start + 1)
    def _():
        dec_acc[...], enc_acc[...] = tiles(start)

        def add(t, carry):
            d, e = tiles(t)
            dec_acc[...] += d
            enc_acc[...] += e
            return carry

        lax.fori_loop(start + 1, stop, add, 0)
        dec_ref[...] = dec_acc[...].astype(BF16)
        enc_ref[...] = enc_acc[...].astype(BF16)


def gradients(order, tile, first, delta, codes, captured, dpre):
    tokens, features = delta.shape
    blocks = tokens // TB
    groups = tile.shape[0]
    whole = pl.BlockSpec(memory_space=VMEM)
    outside = pl.BlockSpec(memory_space=pltpu.HBM)
    return pl.pallas_call(
        grads_kernel,
        grid_spec=pltpu.PrefetchScalarGridSpec(
            num_scalar_prefetch=3,
            grid=(groups,),
            in_specs=[outside, whole, outside, whole],
            out_specs=[
                pl.BlockSpec((features, LB), lambda i, order, tile, first: (0, tile[i])),
                pl.BlockSpec((LB, features), lambda i, order, tile, first: (tile[i], 0)),
            ],
            scratch_shapes=[
                VMEM((tokens, features), BF16), VMEM((tokens, features), BF16),
                VMEM((LB, features), F32), VMEM((features, LB), F32),
                pltpu.SMEM((blocks,), jnp.int32),
                pltpu.SemaphoreType.DMA((blocks,)), pltpu.SemaphoreType.DMA((blocks,)),
            ],
        ),
        out_shape=[
            jax.ShapeDtypeStruct((features, groups * LB), BF16),
            jax.ShapeDtypeStruct((groups * LB, features), BF16),
        ],
        compiler_params=pltpu.CompilerParams(vmem_limit_bytes=BIG),
        name="gradients",
    )(order, tile, first, delta, codes, captured, dpre)


def local(captured, enc_weight, enc_bias, dec_weight, dec_bias, block_ids, block_counts):
    ids = block_ids.reshape(-1)
    counts = block_counts.reshape(-1)
    pre, bias, live, order, tile, first = partial_pre(ids, counts, captured, enc_weight, enc_bias)
    codes, dpre, delta = middle(ids, pre, bias, live, dec_bias, captured, dec_weight, 16, 4)
    codes, dpre = codes.reshape(-1, LB), dpre.reshape(-1, LB)
    return tuple(gradients(order, tile, first, delta, codes, captured, dpre))


def solution(mesh):
    in_specs = (
        P(None, "tok"),
        P("tok", "lat"),
        P("lat"),
        P("lat", "tok"),
        P("tok"),
        P(None, "lat", None),
        P(None, "lat"),
    )
    out_specs = (P("tok", "lat"), P("lat", "tok"))
    return jax.shard_map(local, mesh=mesh, in_specs=in_specs, out_specs=out_specs, check_vma=False)
```

profile of v0, /device:TPU:0, one launch (start us, length us, event | category | flops | bytes accessed | tf_op | source)
XLA Modules:
  0.0 163.1 jit_solution(726061317776186951)
XLA Ops:
  0.6 0.8 copy.10
  1.4 0.6 reshape.28.ids
  2.0 9.3 %partial_pre.1 = (bf16[2048,128]{1,0:T(8,128)(2,1)}, f32[16,1,128]{2,1,0:T(1,128)}, f32[16,1,128]{2,1,0:T(1,128)}, s32[16]{0:T(128)}, s32[32]{0:T(128)}, /*index=5*/s32[33]{0:T(128)}) custom-call(s32[16]{0:T(128)} %reshape.28.ids, s32[8]{0:T(128)} %bitcast.16, bf16[1024,2048]{1,0:T(8,128)(2,1)} %cap_hbm.3, bf16[2048,4096]{1,0:T(8,128)(2,1)} %refs_1_.1, ...), custom_call_target="tpu_custom_call" | custom-call | tf_op jit(solution)/shard_map/partial_pre/pallas_call | solution.py:93
  11.3 128.0 %middle.1 = (bf16[8,256,128]{2,1,0:T(8,128)(2,1)}, bf16[8,256,128]{2,1,0:T(8,128)(2,1)}, bf16[1024,2048]{1,0:T(8,128)(2,1)}) custom-call(s32[16]{0:T(128)} %reshape.28.ids, bf16[8,256,128]{2,1,0:T(8,128)(2,1)} %bitcast.12, f32[16,1,128]{2,1,0:T(1,128)} %get-tuple-element.15.bias_ref, f32[16,1,128]{2,1,0:T(1,128)} %get-tuple-element.16.live_ref, ...), custom_call_target="tpu_custom_call" | custom-call | tf_op jit(solution)/shard_map/middle/pallas_call | solution.py:373
  139.3 23.8 %gradients.1 = (bf16[2048,4096]{1,0:T(8,128)(2,1)}, bf16[4096,2048]{1,0:T(8,128)(2,1)}) custom-call(s32[16]{0:T(128)} %get-tuple-element.11.order, s32[32]{0:T(128)} %get-tuple-element.12.tile, s32[33]{0:T(128)} %get-tuple-element.13.first, bf16[1024,2048]{1,0:T(8,128)(2,1)} %get-tuple-element.17.delta_hbm, bf16[2048,128]{1,0:T(8,128)(2,1)} %bitcast.10, ...), custom_call_target="tpu_custom_call" | custom-call | tf_op jit(solution)/shard_map/gradients/pallas_call | solution.py:479
where the time goes:
time: 163 us
  Pallas kernels  161 us (99%)
    pallas_call x1, Pallas kernels, middle(): pl.pallas_call(functools.partial(middle_kernel, n, nz, chunk, lag), out_s...  128 us
    pallas_call x1, Pallas kernels, gradients(): pl.pallas_call(grads_kernel, grid_spec=pltpu.PrefetchScalarGridSpec(num_s...  23.8 us
    pallas_call x1, Pallas kernels, partial_pre(): pl.pallas_call(pre_kernel, grid_spec=pltpu.PrefetchScalarGridSpec(num_sca...  9.29 us

commit v1 on v0

v1 whole, which is shorter than its diff:
```python
import functools

import jax
import jax.numpy as jnp
from jax import lax
from jax.experimental import pallas as pl
from jax.experimental.pallas import tpu as pltpu
from jax.sharding import PartitionSpec as P

TB = 128
LB = 128
KS = 2

SCALE_ERR = 0.0625
PENALTY = 0.05
CHUNK = 16
LAG = 4
F32 = jnp.float32
BF16 = jnp.bfloat16
MESH = pl.DeviceIdType.MESH
VMEM = pltpu.VMEM
BIG = 60 * 1024 * 1024


def dot(a, b, ca, cb):
    return lax.dot_general(a, b, (((ca,), (cb,)), ((), ())), preferred_element_type=F32)


def rows_of(b, size):
    return pl.ds(pl.multiple_of(b * size, size), size)


def pre_kernel(ids, counts, cap_hbm, enc_hbm, bias_ref, pre_ref, bsel_ref, live_ref, cap_v, tiles_v, cap_sem, tile_sem):
    blocks = pre_ref.shape[0]

    def loads(b):
        copies = [pltpu.make_async_copy(cap_hbm.at[rows_of(b, TB)], cap_v.at[rows_of(b, TB)], cap_sem.at[b])]
        for k in range(KS):
            copies.append(pltpu.make_async_copy(
                enc_hbm.at[:, rows_of(ids[k, b], LB)], tiles_v.at[b, :, pl.ds(k * LB, LB)], tile_sem.at[b * KS + k]
            ))
        return copies

    def begin(b, carry):
        for copy in loads(b):
            copy.start()
        return carry

    def select(b, carry):
        for k in range(KS):
            bsel_ref[k, b] = bias_ref[ids[k, b]]
            live_ref[k, b] = jnp.full((1, LB), (k < counts[b]).astype(F32), F32)
        return carry

    def work(b, carry):
        for copy in loads(b):
            copy.wait()
        pre = dot(cap_v[rows_of(b, TB)], tiles_v[b], 1, 0).astype(BF16)
        for k in range(KS):
            pre_ref[b, pl.ds(k * TB, TB)] = pre[:, k * LB:(k + 1) * LB]
        return carry

    lax.fori_loop(0, blocks, begin, 0)
    lax.fori_loop(0, blocks, select, 0)
    lax.fori_loop(0, blocks, work, 0)


def partial_pre(ids, counts, captured, enc_weight, enc_bias):
    tokens, features = captured.shape
    blocks = tokens // TB
    whole = pl.BlockSpec(memory_space=VMEM)
    outside = pl.BlockSpec(memory_space=pltpu.HBM)
    scalars = pl.BlockSpec(memory_space=pltpu.SMEM)
    return pl.pallas_call(
        pre_kernel,
        in_specs=[scalars, scalars, outside, outside, whole],
        out_specs=[whole] * 3,
        scratch_shapes=[
            VMEM((tokens, features), BF16), VMEM((blocks, features, KS * LB), BF16),
            pltpu.SemaphoreType.DMA((blocks,)), pltpu.SemaphoreType.DMA((blocks * KS,)),
        ],
        out_shape=[
            jax.ShapeDtypeStruct((blocks, KS * TB, LB), BF16),
            jax.ShapeDtypeStruct((KS, blocks, 1, LB), F32),
            jax.ShapeDtypeStruct((KS, blocks, 1, LB), F32),
        ],
        compiler_params=pltpu.CompilerParams(vmem_limit_bytes=BIG),
        name="partial_pre",
    )(ids, counts, captured, enc_weight, enc_bias.reshape(-1, 1, LB))


def spans(cuts):
    return [(lo, hi) for lo, hi in zip(cuts[:-1], cuts[1:]) if lo < hi]


def middle_kernel(
    n, nz, chunk, lag, first_spans, last_spans,
    ids, pre_ref, bias_ref, live_ref, dbias_ref, cap_hbm, dec_hbm,
    codes_ref, dpre_ref, delta_hbm, capt_hbm,
    cap_v, dec_v, part_v, delta_v, capt_v, up_in, down_in, up_out, down_out,
    pre_in, dc_out, dc_in,
    up_send, up_recv, down_send, down_recv,
    pre_send, pre_recv, code_send, code_recv, dc_send, dc_recv, dp_send, dp_recv,
    load_sem, store_sem, capt_sem,
):
    me = lax.axis_index("tok")
    z = lax.axis_index("lat")
    blocks, rows = pre_ref.shape[0], pre_ref.shape[1]
    share = rows // n
    slot = me * share // TB
    per = TB // chunk
    chunks = blocks * per
    has_low = z > 0
    has_high = z < nz - 1
    inner = jnp.logical_and(has_low, has_high)
    low = jnp.maximum(z - 1, 0)
    high = jnp.minimum(z + 1, nz - 1)

    load_dec = pltpu.make_async_copy(dec_hbm, dec_v, load_sem.at[0])
    load_cap = pltpu.make_async_copy(cap_hbm, cap_v, load_sem.at[1])
    load_dec.start()
    load_cap.start()

    barrier = pltpu.get_barrier_semaphore()
    for d in range(1, n):
        pl.semaphore_signal(barrier, inc=1, device_id={"tok": lax.rem(me + d, n)}, device_id_type=MESH)

    @pl.when(has_low)
    def _():
        pl.semaphore_signal(barrier, inc=1, device_id={"lat": low}, device_id_type=MESH)

    @pl.when(has_high)
    def _():
        pl.semaphore_signal(barrier, inc=1, device_id={"lat": high}, device_id_type=MESH)

    pl.semaphore_wait(barrier, n - 1 + has_low.astype(jnp.int32) + has_high.astype(jnp.int32))

    def share_of(j):
        return rows_of(j, share)

    def scatter(src, dst, send, recv, all_spans, i, d):
        lo, hi = all_spans[i]
        peer = lax.rem(me + d, n)
        at = i * (n - 1) + d - 1
        return pltpu.make_async_remote_copy(
            src_ref=src.at[lo:hi, share_of(peer)], dst_ref=dst.at[d - 1, lo:hi],
            send_sem=send.at[at], recv_sem=recv.at[at], device_id={"tok": peer}, device_id_type=MESH,
        )

    def gather(buf, send, recv, all_spans, i, d, owner):
        lo, hi = all_spans[i]
        at = i * (n - 1) + d - 1
        part = buf.at[lo:hi, share_of(owner)]
        return pltpu.make_async_remote_copy(
            src_ref=part, dst_ref=part, send_sem=send.at[at], recv_sem=recv.at[at],
            device_id={"tok": lax.rem(me + n - d, n)}, device_id_type=MESH,
        )

    def pre_copy(i, d):
        return scatter(pre_ref, pre_in, pre_send, pre_recv, first_spans, i, d)

    def dc_copy(i, d):
        return scatter(dc_out, dc_in, dc_send, dc_recv, last_spans, i, d)

    def code_copy(i, d, owner):
        return gather(codes_ref, code_send, code_recv, first_spans, i, d, owner)

    def dp_copy(i, d, owner):
        return gather(dpre_ref, dp_send, dp_recv, last_spans, i, d, owner)

    def other(d):
        return lax.rem(me + d, n)

    def activate(i):
        lo, hi = first_spans[i]
        total = pre_ref[lo:hi, share_of(me)].astype(F32)
        for d in range(1, n):
            pre_copy(i, d).wait_recv()
            total = total + pre_in[d - 1, lo:hi].astype(F32)
        v = total + bias_ref[slot, lo:hi]
        soft = jnp.maximum(v, 0.0) + jnp.log1p(jnp.exp(-jnp.abs(v)))
        codes_ref[lo:hi, share_of(me)] = (soft * live_ref[slot, lo:hi]).astype(BF16)
        for d in range(1, n):
            code_copy(i, d, me).start()

    def codes_here(i):
        for d in range(1, n):
            code_copy(i, d, other(d)).wait_recv()

    def slopes(i):
        lo, hi = last_spans[i]
        total = dc_out[lo:hi, share_of(me)].astype(F32)
        for d in range(1, n):
            dc_copy(i, d).wait_recv()
            total = total + dc_in[d - 1, lo:hi].astype(F32)
        rate = 1.0 - jnp.exp(-codes_ref[lo:hi, share_of(me)].astype(F32))
        dpre_ref[lo:hi, share_of(me)] = ((total + PENALTY) * rate).astype(BF16)
        for d in range(1, n):
            dp_copy(i, d, me).start()

    for i in range(len(first_spans)):
        for d in range(1, n):
            pre_copy(i, d).start()
    activate(0)
    load_dec.wait()
    codes_here(0)

    def chunk_rows(c):
        return rows_of(c, chunk)

    def line_copy(src, dst, send, recv, c, dev):
        return pltpu.make_async_remote_copy(
            src_ref=src.at[chunk_rows(c)], dst_ref=dst.at[chunk_rows(c)], send_sem=send.at[c], recv_sem=recv.at[c],
            device_id={"lat": dev}, device_id_type=MESH,
        )

    def up(c):
        return line_copy(up_out, up_in, up_send, up_recv, c, high)

    def up_first(c):
        return line_copy(part_v, up_in, up_send, up_recv, c, high)

    def down(c):
        return line_copy(down_out, down_in, down_send, down_recv, c, low)

    def down_first(c):
        return line_copy(part_v, down_in, down_send, down_recv, c, low)

    def dec_tile(b):
        return jnp.concatenate([dec_v[ids[k, b]] for k in range(KS)], axis=0)

    def make_part(b):
        tiles = [codes_ref[b, pl.ds(k * TB, TB)] for k in range(KS)]
        part_v[rows_of(b, TB)] = dot(jnp.concatenate(tiles, axis=1), dec_tile(b), 1, 0).astype(BF16)

    def delta_copy(b):
        return pltpu.make_async_copy(delta_v.at[rows_of(b, TB)], delta_hbm.at[rows_of(b, TB)], store_sem.at[b])

    def capt_copy(b):
        return pltpu.make_async_copy(capt_v.at[b], capt_hbm.at[b], capt_sem.at[b])

    up_delay = lag * z
    down_delay = lag * (nz - 1 - z)
    first_delay = jnp.minimum(up_delay, down_delay)
    last_delay = jnp.maximum(up_delay, down_delay)

    def step(t, carry):
        cf = t - first_delay
        cu = t - up_delay
        cd = t - down_delay
        cl = t - last_delay
        stage = jnp.maximum(cf, 0) // per
        fresh = jnp.logical_and(cf >= 0, cf < chunks)

        @pl.when(jnp.logical_and(fresh, lax.rem(jnp.maximum(cf, 0), per) == 0))
        def _():
            for i in range(1, len(first_spans)):
                @pl.when(stage == first_spans[i][0])
                def _():
                    codes_here(i)

            make_part(stage)

        for i in range(1, len(first_spans)):
            @pl.when(cf == first_spans[i - 1][1] * per - per // 2 - 1)
            def _():
                activate(i)

        @pl.when(jnp.logical_and(cu >= 0, cu < chunks))
        def _():
            @pl.when(has_low)
            def _():
                up(cu).wait_recv()

                @pl.when(has_high)
                def _():
                    up_out[chunk_rows(cu)] = (
                        up_in[chunk_rows(cu)].astype(F32) + part_v[chunk_rows(cu)].astype(F32)
                    ).astype(BF16)
                    up(cu).start()

            @pl.when(jnp.logical_not(has_low))
            def _():
                up_first(cu).start()

        @pl.when(jnp.logical_and(cd >= 0, cd < chunks))
        def _():
            @pl.when(has_high)
            def _():
                down(cd).wait_recv()

                @pl.when(has_low)
                def _():
                    down_out[chunk_rows(cd)] = (
                        down_in[chunk_rows(cd)].astype(F32) + part_v[chunk_rows(cd)].astype(F32)
                    ).astype(BF16)
                    down(cd).start()

            @pl.when(jnp.logical_not(has_high))
            def _():
                down_first(cd).start()

        @pl.when(cf == 0)
        def _():
            load_cap.wait()

        @pl.when(jnp.logical_and(fresh, lax.rem(jnp.maximum(cf, 0), per) == per // 2))
        def _():
            capt_v[stage] = cap_v[rows_of(stage, TB)].T
            capt_copy(stage).start()

        @pl.when(jnp.logical_and(cl >= 0, cl < chunks))
        def _():
            at = chunk_rows(cl)
            here = part_v[at].astype(F32) + dbias_ref[...] - cap_v[at].astype(F32)

            @pl.when(inner)
            def _():
                both = up_in[at].astype(F32) + down_in[at].astype(F32)
                delta_v[at] = (SCALE_ERR * (here + both)).astype(BF16)

            @pl.when(jnp.logical_not(has_low))
            def _():
                delta_v[at] = (SCALE_ERR * (here + down_in[at].astype(F32))).astype(BF16)

            @pl.when(jnp.logical_not(has_high))
            def _():
                delta_v[at] = (SCALE_ERR * (here + up_in[at].astype(F32))).astype(BF16)

            done = cl // per

            @pl.when(lax.rem(cl, per) == per - 1)
            def _():
                value = dot(delta_v[rows_of(done, TB)], dec_tile(done), 1, 1).astype(BF16)
                for k in range(KS):
                    dc_out[done, pl.ds(k * TB, TB)] = value[:, k * LB:(k + 1) * LB]
                delta_copy(done).start()

                for i in range(len(last_spans)):
                    @pl.when(done == last_spans[i][1] - 1)
                    def _():
                        for d in range(1, n):
                            dc_copy(i, d).start()

            for i in range(len(last_spans) - 1):
                @pl.when(cl == last_spans[i][1] * per - 1 + per // 2)
                def _():
                    slopes(i)

        return carry

    lax.fori_loop(0, chunks + lag * (nz - 1), step, 0)

    slopes(len(last_spans) - 1)

    def drain(c, carry):
        @pl.when(has_high)
        def _():
            up(c).wait_send()

        @pl.when(has_low)
        def _():
            down(c).wait_send()

        return carry

    lax.fori_loop(0, chunks, drain, 0)

    def stored(b, carry):
        delta_copy(b).wait()
        capt_copy(b).wait()
        return carry

    lax.fori_loop(0, blocks, stored, 0)
    for i in range(len(first_spans)):
        for d in range(1, n):
            pre_copy(i, d).wait_send()
            code_copy(i, d, me).wait_send()
    for i in range(len(last_spans)):
        for d in range(1, n):
            dc_copy(i, d).wait_send()
            dp_copy(i, d, me).wait_send()
            dp_copy(i, d, other(d)).wait_recv()


def middle(ids, pre, bias, live, dec_bias, captured, dec_weight, chunk, lag):
    n = lax.axis_size("tok")
    nz = lax.axis_size("lat")
    tokens, features = captured.shape
    blocks, rows, _ = pre.shape
    lat_dev = dec_weight.shape[0]
    chunks = tokens // chunk
    first_spans = spans([0, 1, blocks])
    last_spans = spans([0, max(blocks - 2, 0), max(blocks - 1, 0), blocks])
    whole = pl.BlockSpec(memory_space=VMEM)
    outside = pl.BlockSpec(memory_space=pltpu.HBM)
    sems = lambda count: [pltpu.SemaphoreType.DMA((count,))]
    wide = VMEM((tokens, features), BF16)
    shares = VMEM((n - 1, blocks, rows // n, LB), BF16)
    return pl.pallas_call(
        functools.partial(middle_kernel, n, nz, chunk, lag, first_spans, last_spans),
        out_shape=[
            jax.ShapeDtypeStruct((blocks, rows, LB), BF16),
            jax.ShapeDtypeStruct((blocks, rows, LB), BF16),
            jax.ShapeDtypeStruct((tokens, features), BF16),
            jax.ShapeDtypeStruct((blocks, features, TB), BF16),
        ],
        in_specs=[pl.BlockSpec(memory_space=pltpu.SMEM)] + [whole] * 4 + [outside] * 2,
        out_specs=[whole, whole, outside, outside],
        scratch_shapes=[wide, VMEM((lat_dev // LB, LB, features), BF16), wide, wide, VMEM((blocks, features, TB), BF16)]
        + [wide] * 4 + [shares, VMEM((blocks, rows, LB), BF16), shares]
        + sems(chunks) * 4 + sems((n - 1) * len(first_spans)) * 4 + sems((n - 1) * len(last_spans)) * 4
        + sems(2) + sems(blocks) * 2,
        compiler_params=pltpu.CompilerParams(
            collective_id=0, has_side_effects=True, vmem_limit_bytes=BIG
        ),
        name="middle",
    )(
        ids, pre, bias, live, dec_bias.reshape(1, features), captured,
        dec_weight.reshape(-1, LB, features),
    )


def grads_kernel(
    ids, delta_hbm, capt_hbm, codes_ref, dpre_ref,
    enc_hbm, dec_hbm, delta_v, capt_v, zero_e, zero_d, out_e, out_d, acc_e, acc_d,
    members, seen, place, spare, delta_sem, capt_sem, enc_sem, dec_sem,
):
    blocks = capt_v.shape[0]
    groups = members.shape[0]

    def loads(b):
        return (
            pltpu.make_async_copy(delta_hbm.at[rows_of(b, TB)], delta_v.at[rows_of(b, TB)], delta_sem.at[b]),
            pltpu.make_async_copy(capt_hbm.at[b], capt_v.at[b], capt_sem.at[b]),
        )

    def enc_copy(src, g):
        return pltpu.make_async_copy(src, enc_hbm.at[:, rows_of(g, LB)], enc_sem.at[g])

    def dec_copy(src, g):
        return pltpu.make_async_copy(src, dec_hbm.at[rows_of(g, LB)], dec_sem.at[g])

    def begin(b, carry):
        for copy in loads(b):
            copy.start()
        return carry

    def clear(g, carry):
        members[g] = 0
        seen[g] = 0
        return carry

    def count(b, carry):
        for k in range(KS):
            members[ids[k, b]] += 1
        return carry

    def blank(g, carry):
        @pl.when(members[g] == 0)
        def _():
            enc_copy(zero_e, g).start()
            dec_copy(zero_d, g).start()

        return carry

    lax.fori_loop(0, blocks, begin, 0)
    zero_e[...] = jnp.zeros(zero_e.shape, BF16)
    zero_d[...] = jnp.zeros(zero_d.shape, BF16)
    lax.fori_loop(0, groups, clear, 0)
    lax.fori_loop(0, blocks, count, 0)
    lax.fori_loop(0, groups, blank, 0)
    spare[0] = 0

    def work(b, carry):
        for copy in loads(b):
            copy.wait()
        for k in range(KS):
            g = ids[k, b]
            s = b * KS + k
            total = members[g]
            before = seen[g]
            seen[g] = before + 1

            def enc_tile():
                return dot(capt_v[b], dpre_ref[b, pl.ds(k * TB, TB)], 1, 0)

            def dec_tile():
                return dot(codes_ref[b, pl.ds(k * TB, TB)], delta_v[rows_of(b, TB)], 0, 0)

            @pl.when(total == 1)
            def _():
                out_e[s] = enc_tile().astype(BF16)
                out_d[s] = dec_tile().astype(BF16)

            @pl.when(total > 1)
            def _():
                @pl.when(before == 0)
                def _():
                    at = spare[0]
                    spare[0] = at + 1
                    place[g] = at
                    acc_e[at] = enc_tile()
                    acc_d[at] = dec_tile()

                @pl.when(before > 0)
                def _():
                    at = place[g]
                    e = acc_e[at] + enc_tile()
                    d = acc_d[at] + dec_tile()

                    @pl.when(before + 1 < total)
                    def _():
                        acc_e[at] = e
                        acc_d[at] = d

                    @pl.when(before + 1 == total)
                    def _():
                        out_e[s] = e.astype(BF16)
                        out_d[s] = d.astype(BF16)

            @pl.when(before + 1 == total)
            def _():
                enc_copy(out_e.at[s], g).start()
                dec_copy(out_d.at[s], g).start()

        return carry

    lax.fori_loop(0, blocks, work, 0)

    def finish(g, carry):
        enc_copy(zero_e, g).wait()
        dec_copy(zero_d, g).wait()
        return carry

    lax.fori_loop(0, groups, finish, 0)


def gradients(ids, delta, capt, codes, dpre, groups):
    tokens, features = delta.shape
    blocks = tokens // TB
    slots = blocks * KS
    whole = pl.BlockSpec(memory_space=VMEM)
    outside = pl.BlockSpec(memory_space=pltpu.HBM)
    shared = max(min(slots // 2, groups), 1)
    return pl.pallas_call(
        grads_kernel,
        in_specs=[pl.BlockSpec(memory_space=pltpu.SMEM), outside, outside, whole, whole],
        out_specs=[outside, outside],
        scratch_shapes=[
            VMEM((tokens, features), BF16), VMEM((blocks, features, TB), BF16),
            VMEM((features, LB), BF16), VMEM((LB, features), BF16),
            VMEM((slots, features, LB), BF16), VMEM((slots, LB, features), BF16),
            VMEM((shared, features, LB), F32), VMEM((shared, LB, features), F32),
            pltpu.SMEM((groups,), jnp.int32), pltpu.SMEM((groups,), jnp.int32),
            pltpu.SMEM((groups,), jnp.int32), pltpu.SMEM((1,), jnp.int32),
            pltpu.SemaphoreType.DMA((blocks,)), pltpu.SemaphoreType.DMA((blocks,)),
            pltpu.SemaphoreType.DMA((groups,)), pltpu.SemaphoreType.DMA((groups,)),
        ],
        out_shape=[
            jax.ShapeDtypeStruct((features, groups * LB), BF16),
            jax.ShapeDtypeStruct((groups * LB, features), BF16),
        ],
        compiler_params=pltpu.CompilerParams(vmem_limit_bytes=BIG),
        name="gradients",
    )(ids, delta, capt, codes, dpre)


def local(captured, enc_weight, enc_bias, dec_weight, dec_bias, block_ids, block_counts):
    ids = block_ids.transpose(1, 2, 0).reshape(KS, -1)
    counts = block_counts.reshape(-1)
    pre, bias, live = partial_pre(ids, counts, captured, enc_weight, enc_bias)
    codes, dpre, delta, capt = middle(ids, pre, bias, live, dec_bias, captured, dec_weight, CHUNK, LAG)
    return tuple(gradients(ids, delta, capt, codes, dpre, dec_weight.shape[0] // LB))


def solution(mesh):
    in_specs = (
        P(None, "tok"),
        P("tok", "lat"),
        P("lat"),
        P("lat", "tok"),
        P("tok"),
        P(None, "lat", None),
        P(None, "lat"),
    )
    out_specs = (P("tok", "lat"), P("lat", "tok"))
    return jax.shard_map(local, mesh=mesh, in_specs=in_specs, out_specs=out_specs, check_vma=False)
```

time: 163 us -> 150 us (0.920)
  Pallas kernels: 161 us -> 149 us
    pallas_call x3, Pallas kernels: 161 us -> 149 us  [the longest x1 127 us: middle(): pl.pallas_call(functools.partial(middle_kernel, n, nz, chunk, lag, first_...]
where the time goes in v1:
time: 150 us; the launch traced here: 149 us
  Pallas kernels  149 us (99%)
    pallas_call x1, Pallas kernels, middle(): pl.pallas_call(functools.partial(middle_kernel, n, nz, chunk, lag, first_...  127 us
    pallas_call x1, Pallas kernels, gradients(): pl.pallas_call(grads_kernel, in_specs=[pl.BlockSpec(memory_space=pltpu.SM...  15.2 us
    pallas_call x1, Pallas kernels, partial_pre(): pl.pallas_call(pre_kernel, in_specs=[scalars, scalars, outside, outside,...  6.89 us

profile of v1, /device:TPU:0, one launch (start us, length us, event | category | flops | bytes accessed | tf_op | source)
XLA Modules:
  0.0 149.5 jit_solution(10589912966130989823)
XLA Ops:
  0.6 6.9 %partial_pre.1 = (bf16[8,256,128]{2,1,0:T(8,128)(2,1)}, f32[2,8,1,128]{3,2,1,0:T(1,128)}, f32[2,8,1,128]{3,2,1,0:T(1,128)}) custom-call(s32[2,8]{1,0:T(2,128)} %bitcast.9, s32[8]{0:T(128)} %bitcast.13, bf16[1024,2048]{1,0:T(8,128)(2,1)} %cap_hbm.3, bf16[2048,4096]{1,0:T(8,128)(2,1)} %enc_hbm.1, f32[32,1,128]{2,1,0:T(1,128)} %bitcast.8), custom_call_target="tpu_custom_call" | custom-call | tf_op jit(solution)/shard_map/partial_pre/pallas_call | solution.py:74
  7.5 126.8 %middle.1 = (bf16[8,256,128]{2,1,0:T(8,128)(2,1)}, bf16[8,256,128]{2,1,0:T(8,128)(2,1)}, bf16[1024,2048]{1,0:T(8,128)(2,1)}, bf16[8,2048,128]{2,1,0:T(8,128)(2,1)}) custom-call(s32[2,8]{1,0:T(2,128)} %bitcast.10, bf16[8,256,128]{2,1,0:T(8,128)(2,1)} %get-tuple-element.9.pre_ref, f32[2,8,1,128]{3,2,1,0:T(1,128)} %get-tuple-element.10.bias_ref, ...), custom_call_target="tpu_custom_call" | custom-call | tf_op jit(solution)/shard_map/middle/pallas_call | solution.py:400
  134.3 15.2 %gradients.1 = (bf16[2048,4096]{1,0:T(8,128)(2,1)}, bf16[4096,2048]{1,0:T(8,128)(2,1)}) custom-call(s32[2,8]{1,0:T(2,128)} %bitcast.11, bf16[1024,2048]{1,0:T(8,128)(2,1)} %get-tuple-element.12.delta_hbm, bf16[8,2048,128]{2,1,0:T(8,128)(2,1)} %get-tuple-element.13.capt_hbm, bf16[8,256,128]{2,1,0:T(8,128)(2,1)} %get-tuple-element.14.codes_ref, ...), custom_call_target="tpu_custom_call" | custom-call | tf_op jit(solution)/shard_map/gradients/pallas_call | solution.py:546

commit v2 on v1

--- a/solution.py
+++ b/solution.py
@@ -14,12 +14,14 @@
 SCALE_ERR = 0.0625
 PENALTY = 0.05
 CHUNK = 16
-LAG = 4
+LAG = 3
 F32 = jnp.float32
 BF16 = jnp.bfloat16
 MESH = pl.DeviceIdType.MESH
 VMEM = pltpu.VMEM
-BIG = 60 * 1024 * 1024
+BIG = 52 * 1024 * 1024
+MIDDLE = 43 * 1024 * 1024
+LAST = 36 * 1024 * 1024
 
 
 def dot(a, b, ca, cb):
@@ -96,12 +98,12 @@
 def middle_kernel(
     n, nz, chunk, lag, first_spans, last_spans,
     ids, pre_ref, bias_ref, live_ref, dbias_ref, cap_hbm, dec_hbm,
-    codes_ref, dpre_ref, delta_hbm, capt_hbm,
-    cap_v, dec_v, part_v, delta_v, capt_v, up_in, down_in, up_out, down_out,
+    codes_ref, dpre_ref, delta_v, capt_v,
+    cap_v, dec_v, part_v, up_in, down_in, up_out, down_out,
     pre_in, dc_out, dc_in,
     up_send, up_recv, down_send, down_recv,
     pre_send, pre_recv, code_send, code_recv, dc_send, dc_recv, dp_send, dp_recv,
-    load_sem, store_sem, capt_sem,
+    load_sem,
 ):
     me = lax.axis_index("tok")
     z = lax.axis_index("lat")
@@ -119,7 +121,6 @@
     load_dec = pltpu.make_async_copy(dec_hbm, dec_v, load_sem.at[0])
     load_cap = pltpu.make_async_copy(cap_hbm, cap_v, load_sem.at[1])
     load_dec.start()
-    load_cap.start()
 
     barrier = pltpu.get_barrier_semaphore()
     for d in range(1, n):
@@ -198,11 +199,14 @@
         for d in range(1, n):
             dp_copy(i, d, me).start()
 
-    for i in range(len(first_spans)):
+    for d in range(1, n):
+        pre_copy(0, d).start()
+    activate(0)
+    for i in range(1, len(first_spans)):
         for d in range(1, n):
             pre_copy(i, d).start()
-    activate(0)
     load_dec.wait()
+    load_cap.start()
     codes_here(0)
 
     def chunk_rows(c):
@@ -232,12 +236,6 @@
     def make_part(b):
         tiles = [codes_ref[b, pl.ds(k * TB, TB)] for k in range(KS)]
         part_v[rows_of(b, TB)] = dot(jnp.concatenate(tiles, axis=1), dec_tile(b), 1, 0).astype(BF16)
-
-    def delta_copy(b):
-        return pltpu.make_async_copy(delta_v.at[rows_of(b, TB)], delta_hbm.at[rows_of(b, TB)], store_sem.at[b])
-
-    def capt_copy(b):
-        return pltpu.make_async_copy(capt_v.at[b], capt_hbm.at[b], capt_sem.at[b])
 
     up_delay = lag * z
     down_delay = lag * (nz - 1 - z)
@@ -307,7 +305,6 @@
         @pl.when(jnp.logical_and(fresh, lax.rem(jnp.maximum(cf, 0), per) == per // 2))
         def _():
             capt_v[stage] = cap_v[rows_of(stage, TB)].T
-            capt_copy(stage).start()
 
         @pl.when(jnp.logical_and(cl >= 0, cl < chunks))
         def _():
@@ -334,7 +331,6 @@
                 value = dot(delta_v[rows_of(done, TB)], dec_tile(done), 1, 1).astype(BF16)
                 for k in range(KS):
                     dc_out[done, pl.ds(k * TB, TB)] = value[:, k * LB:(k + 1) * LB]
-                delta_copy(done).start()
 
                 for i in range(len(last_spans)):
                     @pl.when(done == last_spans[i][1] - 1)
@@ -366,12 +362,6 @@
 
     lax.fori_loop(0, chunks, drain, 0)
 
-    def stored(b, carry):
-        delta_copy(b).wait()
-        capt_copy(b).wait()
-        return carry
-
-    lax.fori_loop(0, blocks, stored, 0)
     for i in range(len(first_spans)):
         for d in range(1, n):
             pre_copy(i, d).wait_send()
@@ -406,13 +396,13 @@
             jax.ShapeDtypeStruct((blocks, features, TB), BF16),
         ],
         in_specs=[pl.BlockSpec(memory_space=pltpu.SMEM)] + [whole] * 4 + [outside] * 2,
-        out_specs=[whole, whole, outside, outside],
-        scratch_shapes=[wide, VMEM((lat_dev // LB, LB, features), BF16), wide, wide, VMEM((blocks, features, TB), BF16)]
+        out_specs=[whole] * 4,
+        scratch_shapes=[wide, VMEM((lat_dev // LB, LB, features), BF16), wide]
         + [wide] * 4 + [shares, VMEM((blocks, rows, LB), BF16), shares]
         + sems(chunks) * 4 + sems((n - 1) * len(first_spans)) * 4 + sems((n - 1) * len(last_spans)) * 4
-        + sems(2) + sems(blocks) * 2,
+        + sems(2),
         compiler_params=pltpu.CompilerParams(
-            collective_id=0, has_side_effects=True, vmem_limit_bytes=BIG
+            collective_id=0, has_side_effects=True, vmem_limit_bytes=MIDDLE
         ),
         name="middle",
     )(
@@ -422,29 +412,18 @@
 
 
 def grads_kernel(
-    ids, delta_hbm, capt_hbm, codes_ref, dpre_ref,
-    enc_hbm, dec_hbm, delta_v, capt_v, zero_e, zero_d, out_e, out_d, acc_e, acc_d,
-    members, seen, place, spare, delta_sem, capt_sem, enc_sem, dec_sem,
+    ids, delta_v, capt_v, codes_ref, dpre_ref,
+    enc_hbm, dec_hbm, zero_e, zero_d, out_e, out_d, acc_e, acc_d,
+    members, seen, place, spare, enc_sem, dec_sem,
 ):
     blocks = capt_v.shape[0]
     groups = members.shape[0]
 
-    def loads(b):
-        return (
-            pltpu.make_async_copy(delta_hbm.at[rows_of(b, TB)], delta_v.at[rows_of(b, TB)], delta_sem.at[b]),
-            pltpu.make_async_copy(capt_hbm.at[b], capt_v.at[b], capt_sem.at[b]),
-        )
-
     def enc_copy(src, g):
         return pltpu.make_async_copy(src, enc_hbm.at[:, rows_of(g, LB)], enc_sem.at[g])
 
     def dec_copy(src, g):
         return pltpu.make_async_copy(src, dec_hbm.at[rows_of(g, LB)], dec_sem.at[g])
-
-    def begin(b, carry):
-        for copy in loads(b):
-            copy.start()
-        return carry
 
     def clear(g, carry):
         members[g] = 0
@@ -464,7 +443,6 @@
 
         return carry
 
-    lax.fori_loop(0, blocks, begin, 0)
     zero_e[...] = jnp.zeros(zero_e.shape, BF16)
     zero_d[...] = jnp.zeros(zero_d.shape, BF16)
     lax.fori_loop(0, groups, clear, 0)
@@ -473,8 +451,6 @@
     spare[0] = 0
 
     def work(b, carry):
-        for copy in loads(b):
-            copy.wait()
         for k in range(KS):
             g = ids[k, b]
             s = b * KS + k
@@ -545,23 +521,21 @@
     shared = max(min(slots // 2, groups), 1)
     return pl.pallas_call(
         grads_kernel,
-        in_specs=[pl.BlockSpec(memory_space=pltpu.SMEM), outside, outside, whole, whole],
+        in_specs=[pl.BlockSpec(memory_space=pltpu.SMEM)] + [whole] * 4,
         out_specs=[outside, outside],
         scratch_shapes=[
-            VMEM((tokens, features), BF16), VMEM((blocks, features, TB), BF16),
             VMEM((features, LB), BF16), VMEM((LB, features), BF16),
             VMEM((slots, features, LB), BF16), VMEM((slots, LB, features), BF16),
             VMEM((shared, features, LB), F32), VMEM((shared, LB, features), F32),
             pltpu.SMEM((groups,), jnp.int32), pltpu.SMEM((groups,), jnp.int32),
             pltpu.SMEM((groups,), jnp.int32), pltpu.SMEM((1,), jnp.int32),
-            pltpu.SemaphoreType.DMA((blocks,)), pltpu.SemaphoreType.DMA((blocks,)),
             pltpu.SemaphoreType.DMA((groups,)), pltpu.SemaphoreType.DMA((groups,)),
         ],
         out_shape=[
             jax.ShapeDtypeStruct((features, groups * LB), BF16),
             jax.ShapeDtypeStruct((groups * LB, features), BF16),
         ],
-        compiler_params=pltpu.CompilerParams(vmem_limit_bytes=BIG),
+        compiler_params=pltpu.CompilerParams(vmem_limit_bytes=LAST),
         name="gradients",
     )(ids, delta, capt, codes, dpre)
 

time: 150 us -> 144 us (0.960)
  Pallas kernels: 149 us -> 141 us
  local copies, waits for them, and re-layouts: 0 us -> 2.05 us
    pallas_call x1, Pallas kernels: 127 us -> 123 us  [middle(): pl.pallas_call(functools.partial(middle_kernel, n, nz, chunk, lag, first_...]
    pallas_call x1, Pallas kernels: 15.2 us -> 12.5 us  [gradients(): pl.pallas_call(grads_kernel, in_specs=[pl.BlockSpec(memory_space=pltpu.SM...]
    unnamed x0 -> x8, local copies, waits for them, and re-layouts: none -> 2.05 us
where the time goes in v2:
time: 144 us
  Pallas kernels  141 us (98%)
  local copies, waits for them, and re-layouts  2.05 us (1%)
    pallas_call x1, Pallas kernels, middle(): pl.pallas_call(functools.partial(middle_kernel, n, nz, chunk, lag, first_...  123 us
    pallas_call x1, Pallas kernels, gradients(): pl.pallas_call(grads_kernel, in_specs=[pl.BlockSpec(memory_space=pltpu.SM...  12.5 us
    pallas_call x1, Pallas kernels, partial_pre(): pl.pallas_call(pre_kernel, in_specs=[scalars, scalars, outside, outside,...  5.92 us

profile of v2, /device:TPU:0, one launch (start us, length us, event | category | flops | bytes accessed | tf_op | source)
XLA Modules:
  0.0 144.1 jit_solution(4591796459947495543)
XLA Ops:
  0.6 0.0 copy-start.2
  0.6 0.0 copy-start
  0.7 0.7 copy-done
  1.4 0.0 copy-start.1
  1.4 0.7 copy-done.1
  2.0 0.0 copy-start.3
  2.0 0.7 copy-done.3
  2.7 5.9 %partial_pre.1 = (bf16[8,256,128]{2,1,0:T(8,128)(2,1)S(1)}, f32[2,8,1,128]{3,2,1,0:T(1,128)S(1)}, f32[2,8,1,128]{3,2,1,0:T(1,128)S(1)}) custom-call(s32[2,8]{1,0:T(2,128)S(1)} %bitcast.8, s32[8]{0:T(128)S(1)} %bitcast.12, bf16[1024,2048]{1,0:T(8,128)(2,1)} %cap_hbm.3, bf16[2048,4096]{1,0:T(8,128)(2,1)} %enc_hbm.1, f32[32,1,128]{2,1,0:T(1,128)S(1)} %bitcast.7), custom_call_target="tpu_custom_call" | custom-call | tf_op jit(solution)/shard_map/partial_pre/pallas_call | solution.py:76
  8.6 0.0 copy-done.2
  8.6 122.9 %middle.1 = (bf16[8,256,128]{2,1,0:T(8,128)(2,1)S(1)}, bf16[8,256,128]{2,1,0:T(8,128)(2,1)S(1)}, bf16[1024,2048]{1,0:T(8,128)(2,1)S(1)}, bf16[8,2048,128]{2,1,0:T(8,128)(2,1)S(1)}) custom-call(s32[2,8]{1,0:T(2,128)S(1)} %bitcast.9, bf16[8,256,128]{2,1,0:T(8,128)(2,1)S(1)} %get-tuple-element.9.pre_ref, f32[2,8,1,128]{3,2,1,0:T(1,128)S(1)} %get-tuple-element.10.bias_ref, ...), custom_call_target="tpu_custom_call" | custom-call | tf_op jit(solution)/shard_map/middle/pallas_call | solution.py:390
  131.5 12.5 %gradients.1 = (bf16[2048,4096]{1,0:T(8,128)(2,1)}, bf16[4096,2048]{1,0:T(8,128)(2,1)}) custom-call(s32[2,8]{1,0:T(2,128)S(1)} %bitcast.10, bf16[1024,2048]{1,0:T(8,128)(2,1)S(1)} %get-tuple-element.12.delta_v, bf16[8,2048,128]{2,1,0:T(8,128)(2,1)S(1)} %get-tuple-element.13.capt_v, bf16[8,256,128]{2,1,0:T(8,128)(2,1)S(1)} %get-tuple-element.14.codes_ref, ...), custom_call_target="tpu_custom_call" | custom-call | tf_op jit(solution)/shard_map/gradients/pallas_call | solution.py:522
Async XLA Ops:
  0.6 8.0 %copy-start.2 = (f32[2048]{0:T(1024)S(1)}, f32[2048]{0:T(1024)}, u32[]{:S(2)}) copy-start(f32[2048]{0:T(1024)} %param.11) | copy-start | bytes 24580
  0.6 0.7 copy-start
  1.4 0.7 copy-start.1
  2.0 0.7 copy-start.3

commit v3 on v2

--- a/solution.py
+++ b/solution.py
@@ -32,8 +32,44 @@
     return pl.ds(pl.multiple_of(b * size, size), size)
 
 
-def pre_kernel(ids, counts, cap_hbm, enc_hbm, bias_ref, pre_ref, bsel_ref, live_ref, cap_v, tiles_v, cap_sem, tile_sem):
+def pre_kernel(
+    ids, counts, cap_hbm, enc_hbm, bias_ref, pre_ref, bsel_ref, live_ref, egrad_hbm, dgrad_hbm,
+    cap_v, tiles_v, zero_e, zero_d, members, cap_sem, tile_sem, enc_sem, dec_sem,
+):
     blocks = pre_ref.shape[0]
+    groups = members.shape[0]
+
+    def clear(g, carry):
+        members[g] = 0
+        return carry
+
+    def count(b, carry):
+        for k in range(KS):
+            members[ids[k, b]] += 1
+        return carry
+
+    def blanks(g):
+        return (
+            pltpu.make_async_copy(zero_e, egrad_hbm.at[:, rows_of(g, LB)], enc_sem.at[g]),
+            pltpu.make_async_copy(zero_d, dgrad_hbm.at[rows_of(g, LB)], dec_sem.at[g]),
+        )
+
+    def blank(g, carry):
+        @pl.when(members[g] == 0)
+        def _():
+            for copy in blanks(g):
+                copy.start()
+
+        return carry
+
+    def blanked(g, carry):
+        @pl.when(members[g] == 0)
+        def _():
+            for copy in blanks(g):
+                copy.wait()
+
+        return carry
+
 
     def loads(b):
         copies = [pltpu.make_async_copy(cap_hbm.at[rows_of(b, TB)], cap_v.at[rows_of(b, TB)], cap_sem.at[b])]
@@ -63,28 +99,39 @@
         return carry
 
     lax.fori_loop(0, blocks, begin, 0)
+    zero_e[...] = jnp.zeros(zero_e.shape, BF16)
+    zero_d[...] = jnp.zeros(zero_d.shape, BF16)
+    lax.fori_loop(0, groups, clear, 0)
+    lax.fori_loop(0, blocks, count, 0)
+    lax.fori_loop(0, groups, blank, 0)
     lax.fori_loop(0, blocks, select, 0)
     lax.fori_loop(0, blocks, work, 0)
+    lax.fori_loop(0, groups, blanked, 0)
 
 
 def partial_pre(ids, counts, captured, enc_weight, enc_bias):
     tokens, features = captured.shape
     blocks = tokens // TB
+    groups = enc_weight.shape[1] // LB
     whole = pl.BlockSpec(memory_space=VMEM)
     outside = pl.BlockSpec(memory_space=pltpu.HBM)
     scalars = pl.BlockSpec(memory_space=pltpu.SMEM)
     return pl.pallas_call(
         pre_kernel,
         in_specs=[scalars, scalars, outside, outside, whole],
-        out_specs=[whole] * 3,
+        out_specs=[whole] * 3 + [outside] * 2,
         scratch_shapes=[
             VMEM((tokens, features), BF16), VMEM((blocks, features, KS * LB), BF16),
+            VMEM((features, LB), BF16), VMEM((LB, features), BF16), pltpu.SMEM((groups,), jnp.int32),
             pltpu.SemaphoreType.DMA((blocks,)), pltpu.SemaphoreType.DMA((blocks * KS,)),
+            pltpu.SemaphoreType.DMA((groups,)), pltpu.SemaphoreType.DMA((groups,)),
         ],
         out_shape=[
             jax.ShapeDtypeStruct((blocks, KS * TB, LB), BF16),
             jax.ShapeDtypeStruct((KS, blocks, 1, LB), F32),
             jax.ShapeDtypeStruct((KS, blocks, 1, LB), F32),
+            jax.ShapeDtypeStruct((features, groups * LB), BF16),
+            jax.ShapeDtypeStruct((groups * LB, features), BF16),
         ],
         compiler_params=pltpu.CompilerParams(vmem_limit_bytes=BIG),
         name="partial_pre",
@@ -412,8 +459,8 @@
 
 
 def grads_kernel(
-    ids, delta_v, capt_v, codes_ref, dpre_ref,
-    enc_hbm, dec_hbm, zero_e, zero_d, out_e, out_d, acc_e, acc_d,
+    ids, delta_v, capt_v, codes_ref, dpre_ref, egrad_in, dgrad_in,
+    enc_hbm, dec_hbm, out_e, out_d, acc_e, acc_d,
     members, seen, place, spare, enc_sem, dec_sem,
 ):
     blocks = capt_v.shape[0]
@@ -435,19 +482,8 @@
             members[ids[k, b]] += 1
         return carry
 
-    def blank(g, carry):
-        @pl.when(members[g] == 0)
-        def _():
-            enc_copy(zero_e, g).start()
-            dec_copy(zero_d, g).start()
-
-        return carry
-
-    zero_e[...] = jnp.zeros(zero_e.shape, BF16)
-    zero_d[...] = jnp.zeros(zero_d.shape, BF16)
     lax.fori_loop(0, groups, clear, 0)
     lax.fori_loop(0, blocks, count, 0)
-    lax.fori_loop(0, groups, blank, 0)
     spare[0] = 0
 
     def work(b, carry):
@@ -505,14 +541,17 @@
     lax.fori_loop(0, blocks, work, 0)
 
     def finish(g, carry):
-        enc_copy(zero_e, g).wait()
-        dec_copy(zero_d, g).wait()
+        @pl.when(members[g] > 0)
+        def _():
+            enc_copy(out_e.at[0], g).wait()
+            dec_copy(out_d.at[0], g).wait()
+
         return carry
 
     lax.fori_loop(0, groups, finish, 0)
 
 
-def gradients(ids, delta, capt, codes, dpre, groups):
+def gradients(ids, delta, capt, codes, dpre, egrad, dgrad, groups):
     tokens, features = delta.shape
     blocks = tokens // TB
     slots = blocks * KS
@@ -521,10 +560,10 @@
     shared = max(min(slots // 2, groups), 1)
     return pl.pallas_call(
         grads_kernel,
-        in_specs=[pl.BlockSpec(memory_space=pltpu.SMEM)] + [whole] * 4,
+        in_specs=[pl.BlockSpec(memory_space=pltpu.SMEM)] + [whole] * 4 + [outside] * 2,
         out_specs=[outside, outside],
+        input_output_aliases={5: 0, 6: 1},
         scratch_shapes=[
-            VMEM((features, LB), BF16), VMEM((LB, features), BF16),
             VMEM((slots, features, LB), BF16), VMEM((slots, LB, features), BF16),
             VMEM((shared, features, LB), F32), VMEM((shared, LB, features), F32),
             pltpu.SMEM((groups,), jnp.int32), pltpu.SMEM((groups,), jnp.int32),
@@ -537,15 +576,15 @@
         ],
         compiler_params=pltpu.CompilerParams(vmem_limit_bytes=LAST),
         name="gradients",
-    )(ids, delta, capt, codes, dpre)
+    )(ids, delta, capt, codes, dpre, egrad, dgrad)
 
 
 def local(captured, enc_weight, enc_bias, dec_weight, dec_bias, block_ids, block_counts):
     ids = block_ids.transpose(1, 2, 0).reshape(KS, -1)
     counts = block_counts.reshape(-1)
-    pre, bias, live = partial_pre(ids, counts, captured, enc_weight, enc_bias)
+    pre, bias, live, egrad, dgrad = partial_pre(ids, counts, captured, enc_weight, enc_bias)
     codes, dpre, delta, capt = middle(ids, pre, bias, live, dec_bias, captured, dec_weight, CHUNK, LAG)
-    return tuple(gradients(ids, delta, capt, codes, dpre, dec_weight.shape[0] // LB))
+    return tuple(gradients(ids, delta, capt, codes, dpre, egrad, dgrad, dec_weight.shape[0] // LB))
 
 
 def solution(mesh):

time: 144 us -> 150 us (1.042)
  Pallas kernels: 141 us -> 147 us
    pallas_call x1, Pallas kernels: 5.92 us -> 13.5 us  [partial_pre(): pl.pallas_call(pre_kernel, in_specs=[scalars, scalars, outside, outside,...]
    pallas_call x1, Pallas kernels: 12.5 us -> 10.2 us  [gradients(): pl.pallas_call(grads_kernel, in_specs=[pl.BlockSpec(memory_space=pltpu.SM...]
where the time goes in v3:
time: 150 us; the launch traced here: 149 us
  Pallas kernels  147 us (98%)
  local copies, waits for them, and re-layouts  2.05 us (1%)
    pallas_call x1, Pallas kernels, middle(): pl.pallas_call(functools.partial(middle_kernel, n, nz, chunk, lag, first_...  123 us
    pallas_call x1, Pallas kernels, partial_pre(): pl.pallas_call(pre_kernel, in_specs=[scalars, scalars, outside, outside,...  13.5 us
    pallas_call x1, Pallas kernels, gradients(): pl.pallas_call(grads_kernel, in_specs=[pl.BlockSpec(memory_space=pltpu.SM...  10.2 us

profile of v3, /device:TPU:0, one launch (start us, length us, event | category | flops | bytes accessed | tf_op | source)
XLA Modules:
  0.0 149.4 jit_solution(21390317743288210)
XLA Ops:
  0.6 0.0 copy-start.2
  0.6 0.0 copy-start
  0.7 0.7 copy-done
  1.4 0.0 copy-start.1
  1.4 0.7 copy-done.1
  2.0 0.0 copy-start.3
  2.0 0.7 copy-done.3
  2.7 13.5 %partial_pre.1 = (bf16[8,256,128]{2,1,0:T(8,128)(2,1)S(1)}, f32[2,8,1,128]{3,2,1,0:T(1,128)S(1)}, f32[2,8,1,128]{3,2,1,0:T(1,128)S(1)}, bf16[2048,4096]{1,0:T(8,128)(2,1)}, bf16[4096,2048]{1,0:T(8,128)(2,1)}) custom-call(s32[2,8]{1,0:T(2,128)S(1)} %bitcast.8, s32[8]{0:T(128)S(1)} %bitcast.12, bf16[1024,2048]{1,0:T(8,128)(2,1)} %cap_hbm.3, ...), custom_call_target="tpu_custom_call" | custom-call | tf_op jit(solution)/shard_map/partial_pre/pallas_call | solution.py:119
  16.3 0.0 copy-done.2
  16.3 122.9 %middle.1 = (bf16[8,256,128]{2,1,0:T(8,128)(2,1)S(1)}, bf16[8,256,128]{2,1,0:T(8,128)(2,1)S(1)}, bf16[1024,2048]{1,0:T(8,128)(2,1)S(1)}, bf16[8,2048,128]{2,1,0:T(8,128)(2,1)S(1)}) custom-call(s32[2,8]{1,0:T(2,128)S(1)} %bitcast.9, bf16[8,256,128]{2,1,0:T(8,128)(2,1)S(1)} %get-tuple-element.11.pre_ref, f32[2,8,1,128]{3,2,1,0:T(1,128)S(1)} %get-tuple-element.12.bias_ref, ...), custom_call_target="tpu_custom_call" | custom-call | tf_op jit(solution)/shard_map/middle/pallas_call | solution.py:437
  139.2 10.2 %gradients.1 = (bf16[2048,4096]{1,0:T(8,128)(2,1)}, bf16[4096,2048]{1,0:T(8,128)(2,1)}) custom-call(s32[2,8]{1,0:T(2,128)S(1)} %bitcast.10, bf16[1024,2048]{1,0:T(8,128)(2,1)S(1)} %get-tuple-element.14.delta_v, bf16[8,2048,128]{2,1,0:T(8,128)(2,1)S(1)} %get-tuple-element.15.capt_v, ...), custom_call_target="tpu_custom_call", output_to_operand_aliasing={{0}: (5, {}), {1}: (6, {})} | custom-call | tf_op jit(solution)/shard_map/gradients/pallas_call | solution.py:561
Async XLA Ops:
  0.6 15.6 %copy-start.2 = (f32[2048]{0:T(1024)S(1)}, f32[2048]{0:T(1024)}, u32[]{:S(2)}) copy-start(f32[2048]{0:T(1024)} %param.11) | copy-start | bytes 24580
  0.6 0.7 copy-start
  1.4 0.7 copy-start.1
  2.0 0.7 copy-start.3

commit v4 on v2

--- a/solution.py
+++ b/solution.py
@@ -32,7 +32,7 @@
     return pl.ds(pl.multiple_of(b * size, size), size)
 
 
-def pre_kernel(ids, counts, cap_hbm, enc_hbm, bias_ref, pre_ref, bsel_ref, live_ref, cap_v, tiles_v, cap_sem, tile_sem):
+def pre_kernel(ids, cap_hbm, enc_hbm, pre_ref, cap_v, tiles_v, cap_sem, tile_sem):
     blocks = pre_ref.shape[0]
 
     def loads(b):
@@ -48,12 +48,6 @@
             copy.start()
         return carry
 
-    def select(b, carry):
-        for k in range(KS):
-            bsel_ref[k, b] = bias_ref[ids[k, b]]
-            live_ref[k, b] = jnp.full((1, LB), (k < counts[b]).astype(F32), F32)
-        return carry
-
     def work(b, carry):
         for copy in loads(b):
             copy.wait()
@@ -63,11 +57,10 @@
         return carry
 
     lax.fori_loop(0, blocks, begin, 0)
-    lax.fori_loop(0, blocks, select, 0)
     lax.fori_loop(0, blocks, work, 0)
 
 
-def partial_pre(ids, counts, captured, enc_weight, enc_bias):
+def partial_pre(ids, captured, enc_weight):
     tokens, features = captured.shape
     blocks = tokens // TB
     whole = pl.BlockSpec(memory_space=VMEM)
@@ -75,20 +68,16 @@
     scalars = pl.BlockSpec(memory_space=pltpu.SMEM)
     return pl.pallas_call(
         pre_kernel,
-        in_specs=[scalars, scalars, outside, outside, whole],
-        out_specs=[whole] * 3,
+        in_specs=[scalars, outside, outside],
+        out_specs=whole,
         scratch_shapes=[
             VMEM((tokens, features), BF16), VMEM((blocks, features, KS * LB), BF16),
             pltpu.SemaphoreType.DMA((blocks,)), pltpu.SemaphoreType.DMA((blocks * KS,)),
         ],
-        out_shape=[
-            jax.ShapeDtypeStruct((blocks, KS * TB, LB), BF16),
-            jax.ShapeDtypeStruct((KS, blocks, 1, LB), F32),
-            jax.ShapeDtypeStruct((KS, blocks, 1, LB), F32),
-        ],
+        out_shape=jax.ShapeDtypeStruct((blocks, KS * TB, LB), BF16),
         compiler_params=pltpu.CompilerParams(vmem_limit_bytes=BIG),
         name="partial_pre",
-    )(ids, counts, captured, enc_weight, enc_bias.reshape(-1, 1, LB))
+    )(ids, captured, enc_weight)
 
 
 def spans(cuts):
@@ -97,9 +86,9 @@
 
 def middle_kernel(
     n, nz, chunk, lag, first_spans, last_spans,
-    ids, pre_ref, bias_ref, live_ref, dbias_ref, cap_hbm, dec_hbm,
+    ids, counts, pre_ref, ebias_ref, dbias_ref, cap_hbm, dec_hbm,
     codes_ref, dpre_ref, delta_v, capt_v,
-    cap_v, dec_v, part_v, up_in, down_in, up_out, down_out,
+    bias_ref, live_ref, cap_v, dec_v, part_v, up_in, down_in, up_out, down_out,
     pre_in, dc_out, dc_in,
     up_send, up_recv, down_send, down_recv,
     pre_send, pre_recv, code_send, code_recv, dc_send, dc_recv, dp_send, dp_recv,
@@ -134,6 +123,12 @@
     def _():
         pl.semaphore_signal(barrier, inc=1, device_id={"lat": high}, device_id_type=MESH)
 
+    def select(b, carry):
+        bias_ref[b] = ebias_ref[ids[slot, b]]
+        live_ref[b] = jnp.full((1, LB), (slot < counts[b]).astype(F32), F32)
+        return carry
+
+    lax.fori_loop(0, blocks, select, 0)
     pl.semaphore_wait(barrier, n - 1 + has_low.astype(jnp.int32) + has_high.astype(jnp.int32))
 
     def share_of(j):
@@ -178,9 +173,9 @@
         for d in range(1, n):
             pre_copy(i, d).wait_recv()
             total = total + pre_in[d - 1, lo:hi].astype(F32)
-        v = total + bias_ref[slot, lo:hi]
+        v = total + bias_ref[lo:hi]
         soft = jnp.maximum(v, 0.0) + jnp.log1p(jnp.exp(-jnp.abs(v)))
-        codes_ref[lo:hi, share_of(me)] = (soft * live_ref[slot, lo:hi]).astype(BF16)
+        codes_ref[lo:hi, share_of(me)] = (soft * live_ref[lo:hi]).astype(BF16)
         for d in range(1, n):
             code_copy(i, d, me).start()
 
@@ -237,6 +232,7 @@
         tiles = [codes_ref[b, pl.ds(k * TB, TB)] for k in range(KS)]
         part_v[rows_of(b, TB)] = dot(jnp.concatenate(tiles, axis=1), dec_tile(b), 1, 0).astype(BF16)
 
+    lower = 2 * z < nz
     up_delay = lag * z
     down_delay = lag * (nz - 1 - z)
     first_delay = jnp.minimum(up_delay, down_delay)
@@ -264,22 +260,25 @@
             def _():
                 activate(i)
 
-        @pl.when(jnp.logical_and(cu >= 0, cu < chunks))
-        def _():
-            @pl.when(has_low)
-            def _():
-                up(cu).wait_recv()
-
-                @pl.when(has_high)
-                def _():
-                    up_out[chunk_rows(cu)] = (
-                        up_in[chunk_rows(cu)].astype(F32) + part_v[chunk_rows(cu)].astype(F32)
-                    ).astype(BF16)
-                    up(cu).start()
-
-            @pl.when(jnp.logical_not(has_low))
-            def _():
-                up_first(cu).start()
+        def pass_up():
+            @pl.when(jnp.logical_and(cu >= 0, cu < chunks))
+            def _():
+                @pl.when(has_low)
+                def _():
+                    up(cu).wait_recv()
+
+                    @pl.when(has_high)
+                    def _():
+                        up_out[chunk_rows(cu)] = (
+                            up_in[chunk_rows(cu)].astype(F32) + part_v[chunk_rows(cu)].astype(F32)
+                        ).astype(BF16)
+                        up(cu).start()
+
+                @pl.when(jnp.logical_not(has_low))
+                def _():
+                    up_first(cu).start()
+
+        pl.when(lower)(pass_up)
 
         @pl.when(jnp.logical_and(cd >= 0, cd < chunks))
         def _():
@@ -297,6 +296,8 @@
             @pl.when(jnp.logical_not(has_high))
             def _():
                 down_first(cd).start()
+
+        pl.when(jnp.logical_not(lower))(pass_up)
 
         @pl.when(cf == 0)
         def _():
@@ -373,7 +374,7 @@
             dp_copy(i, d, other(d)).wait_recv()
 
 
-def middle(ids, pre, bias, live, dec_bias, captured, dec_weight, chunk, lag):
+def middle(ids, counts, pre, enc_bias, dec_bias, captured, dec_weight, chunk, lag):
     n = lax.axis_size("tok")
     nz = lax.axis_size("lat")
     tokens, features = captured.shape
@@ -395,9 +396,9 @@
             jax.ShapeDtypeStruct((tokens, features), BF16),
             jax.ShapeDtypeStruct((blocks, features, TB), BF16),
         ],
-        in_specs=[pl.BlockSpec(memory_space=pltpu.SMEM)] + [whole] * 4 + [outside] * 2,
+        in_specs=[pl.BlockSpec(memory_space=pltpu.SMEM)] * 2 + [whole] * 3 + [outside] * 2,
         out_specs=[whole] * 4,
-        scratch_shapes=[wide, VMEM((lat_dev // LB, LB, features), BF16), wide]
+        scratch_shapes=[VMEM((blocks, 1, LB), F32)] * 2 + [wide, VMEM((lat_dev // LB, LB, features), BF16), wide]
         + [wide] * 4 + [shares, VMEM((blocks, rows, LB), BF16), shares]
         + sems(chunks) * 4 + sems((n - 1) * len(first_spans)) * 4 + sems((n - 1) * len(last_spans)) * 4
         + sems(2),
@@ -406,7 +407,7 @@
         ),
         name="middle",
     )(
-        ids, pre, bias, live, dec_bias.reshape(1, features), captured,
+        ids, counts, pre, enc_bias.reshape(-1, 1, LB), dec_bias.reshape(1, features), captured,
         dec_weight.reshape(-1, LB, features),
     )
 
@@ -543,8 +544,8 @@
 def local(captured, enc_weight, enc_bias, dec_weight, dec_bias, block_ids, block_counts):
     ids = block_ids.transpose(1, 2, 0).reshape(KS, -1)
     counts = block_counts.reshape(-1)
-    pre, bias, live = partial_pre(ids, counts, captured, enc_weight, enc_bias)
-    codes, dpre, delta, capt = middle(ids, pre, bias, live, dec_bias, captured, dec_weight, CHUNK, LAG)
+    pre = partial_pre(ids, captured, enc_weight)
+    codes, dpre, delta, capt = middle(ids, counts, pre, enc_bias, dec_bias, captured, dec_weight, CHUNK, LAG)
     return tuple(gradients(ids, delta, capt, codes, dpre, dec_weight.shape[0] // LB))
 
 

time: 144 us -> 143 us (level)
  no operation moved by 1% of the time
where the time goes in v4:
time: 143 us
  Pallas kernels  141 us (99%)
    pallas_call x1, Pallas kernels, middle(): pl.pallas_call(functools.partial(middle_kernel, n, nz, chunk, lag, first_...  123 us
    pallas_call x1, Pallas kernels, gradients(): pl.pallas_call(grads_kernel, in_specs=[pl.BlockSpec(memory_space=pltpu.SM...  12.4 us
    pallas_call x1, Pallas kernels, partial_pre(): pl.pallas_call(pre_kernel, in_specs=[scalars, outside, outside], out_spec...  5.91 us

profile of v4, /device:TPU:0, one launch (start us, length us, event | category | flops | bytes accessed | tf_op | source)
XLA Modules:
  0.0 142.6 jit_solution(5776922979479245800)
XLA Ops:
  0.6 0.0 copy-start
  0.6 0.0 copy-start.1
  0.7 0.7 copy-done.1
  1.3 0.0 copy-start.2
  1.3 0.0 copy-start.3
  1.3 5.9 %partial_pre.1.pre_ref = bf16[8,256,128]{2,1,0:T(8,128)(2,1)S(1)} custom-call(s32[2,8]{1,0:T(2,128)S(1)} %bitcast.8, bf16[1024,2048]{1,0:T(8,128)(2,1)} %cap_hbm.3, bf16[2048,4096]{1,0:T(8,128)(2,1)} %enc_hbm.1), custom_call_target="tpu_custom_call" | custom-call | tf_op jit(solution)/shard_map/partial_pre/pallas_call | solution.py:69
  7.3 0.0 copy-done
  7.3 0.0 copy-done.2
  7.3 0.0 copy-done.3
  7.3 122.9 %middle.1 = (bf16[8,256,128]{2,1,0:T(8,128)(2,1)S(1)}, bf16[8,256,128]{2,1,0:T(8,128)(2,1)S(1)}, bf16[1024,2048]{1,0:T(8,128)(2,1)S(1)}, bf16[8,2048,128]{2,1,0:T(8,128)(2,1)S(1)}) custom-call(s32[2,8]{1,0:T(2,128)S(1)} %bitcast.9, s32[8]{0:T(128)S(1)} %bitcast.12, bf16[8,256,128]{2,1,0:T(8,128)(2,1)S(1)} %partial_pre.1.pre_ref, f32[32,1,128]{2,1,0:T(1,128)S(1)} %bitcast.7, ...), custom_call_target="tpu_custom_call" | custom-call | tf_op jit(solution)/shard_map/middle/pallas_call | solution.py:391
  130.2 12.4 %gradients.1 = (bf16[2048,4096]{1,0:T(8,128)(2,1)}, bf16[4096,2048]{1,0:T(8,128)(2,1)}) custom-call(s32[2,8]{1,0:T(2,128)S(1)} %bitcast.10, bf16[1024,2048]{1,0:T(8,128)(2,1)S(1)} %get-tuple-element.6.delta_v, bf16[8,2048,128]{2,1,0:T(8,128)(2,1)S(1)} %get-tuple-element.7.capt_v, bf16[8,256,128]{2,1,0:T(8,128)(2,1)S(1)} %get-tuple-element.8.codes_ref, ...), custom_call_target="tpu_custom_call" | custom-call | tf_op jit(solution)/shard_map/gradients/pallas_call | solution.py:523
Async XLA Ops:
  0.6 6.6 %copy-start = (f32[4096]{0:T(1024)S(1)}, f32[4096]{0:T(1024)}, u32[]{:S(2)}) copy-start(f32[4096]{0:T(1024)} %param.9) | copy-start | bytes 49156
  0.6 0.7 copy-start.1
  1.3 5.9 %copy-start.2 = (f32[2048]{0:T(1024)S(1)}, f32[2048]{0:T(1024)}, u32[]{:S(2)}) copy-start(f32[2048]{0:T(1024)} %param.11) | copy-start | bytes 24580
  1.3 5.9 %copy-start.3 = (s32[8,1]{0,1:T(1,128)S(1)}, s32[8,1]{0,1:T(1,128)}, u32[]{:S(2)}) copy-start(s32[8,1]{0,1:T(1,128)} %param.13) | copy-start | bytes 100
